TPU v7x, 256 devices: a whole 4x4x8 slice. The times are simulated.
256 devices in a mesh: gx: 16 (over x, y), gy: 8 (over z), gz: 2 (over core).
Axes of the slice: x: 4, y: 4, z: 8, core: 2. Of those that a mesh axis runs over, the one named last changes fastest.
Arguments:
- well_sources: float32 [12288, 64], P(('gx', 'gy'), 'gz'), may hold values from -6 to 6
- well_owner: int32 [12288, 1], P(('gx', 'gy')), may hold values from 0 to 127; in each aligned block of 96 rows (0 to 95, 96 to 191, ...) at most 2 rows name the same one
- well_cell: int32 [12288], P(('gx', 'gy')), may hold values from 0 to 2047
- flow_sign: int32 [3, 64, 256, 1024], P(None, 'gz', 'gx', 'gy'), may hold values from 0 to 7
- courant: float32 [3, 64, 256, 1024], P(None, 'gz', 'gx', 'gy'), may hold values from 0.01 to 0.3
- tracer: float32 [3, 64, 256, 1024], P(None, 'gz', 'gx', 'gy'), may hold values from -6 to 6
Outputs:
- lambda_start: float32 [64, 256, 1024], P('gz', 'gx', 'gy')
- smoothed: float32 [1024, 64, 256], P(('gx', 'gy', 'gz'))
Inputs may be any that keep to these rules, and one draw needn't show every extreme that they name: `well_owner`: among the wells of one index of gx+gy at most 2 name the same owner, a bound that some block of them reaches.
All inputs are finite; a program needn't handle non-finite values.
Results may differ from a plain program's by a relative error of at most 0.00015.
Values sent between devices are 32-bit elements; how exact they have to be, the bound alone decides.
No kernel may reach another device: no remote copies, remote signals or barrier semaphores. Data moves between devices by JAX's collectives and lax.ppermute only.
A program may use at most 128 MiB of HBM per device.

v0:
```python
import math
import jax
import jax.numpy as jnp
from jax import lax
from jax.sharding import PartitionSpec as P

STEPS = 3


def with_halo(block, sides, width):
    for axis, dim in sides:
        count = lax.axis_size(axis)
        forward = [(i, i + 1) for i in range(count - 1)]
        backward = [(target, source) for source, target in forward]
        low = lax.ppermute(
            lax.slice_in_dim(block, block.shape[dim] - width, None, axis=dim), axis, forward
        )
        high = lax.ppermute(lax.slice_in_dim(block, 0, width, axis=dim), axis, backward)
        block = jnp.concatenate([low, block, high], axis=dim)
    return block


def correlation(extent, length):
    places = jnp.arange(extent).astype(jnp.float32)
    spacing = jnp.abs(places[:, None] - places[None, :])
    return jnp.exp(-spacing / length) / math.sqrt(length)


def advance_weights(adjoint, rising_pad, falling_pad, staying):
    padded = with_halo(adjoint, (("gx", 1), ("gy", 2), ("gz", 0)), 1)
    updated = staying * adjoint
    updated = (
        updated
        + rising_pad[0, 1:-1, 2:, 1:-1] * padded[1:-1, 2:, 1:-1]
        + falling_pad[0, 1:-1, :-2, 1:-1] * padded[1:-1, :-2, 1:-1]
    )
    updated = (
        updated
        + rising_pad[1, 1:-1, 1:-1, 2:] * padded[1:-1, 1:-1, 2:]
        + falling_pad[1, 1:-1, 1:-1, :-2] * padded[1:-1, 1:-1, :-2]
    )
    updated = (
        updated
        + rising_pad[2, 2:, 1:-1, 1:-1] * padded[2:, 1:-1, 1:-1]
        + falling_pad[2, :-2, 1:-1, 1:-1] * padded[:-2, 1:-1, 1:-1]
    )
    return updated


def per_device(well_sources, well_owner, well_cell, flow_sign, courant, tracer):
    brick_z, brick_x, brick_y = (courant.shape[1], courant.shape[2], courant.shape[3])
    columns = brick_x * brick_y
    groups = lax.axis_size("gx") * lax.axis_size("gy")
    my_owner = lax.axis_index("gx") * lax.axis_size("gy") + lax.axis_index("gy")
    owners = well_owner[:, 0]
    all_sources, all_owner, all_cell = (
        lax.all_gather(well_sources, ("gx", "gy"), axis=0, tiled=True),
        lax.all_gather(owners, ("gx", "gy"), axis=0, tiled=True),
        lax.all_gather(well_cell, ("gx", "gy"), axis=0, tiled=True),
    )
    target = jnp.where(all_owner == my_owner, all_cell, columns)
    landed = (
        jnp.zeros((brick_z, columns), jnp.float32)
        .at[:, target]
        .add(jnp.transpose(all_sources), mode="drop")
    )
    adjoint = landed.reshape(brick_z, brick_x, brick_y)
    upward = jnp.stack([flow_sign // 1 % 2, flow_sign // 2 % 2, flow_sign // 4 % 2], axis=1).astype(
        jnp.float32
    )
    staying = 1.0 - (courant[0] + courant[1] + courant[2])
    gradient = jnp.zeros((brick_z, brick_x, brick_y), jnp.float32)
    weights = jnp.stack([courant[None] * upward, courant[None] * (1.0 - upward)])
    weight_pad = with_halo(weights, (("gx", 4), ("gy", 5), ("gz", 3)), 1)
    for step in reversed(range(STEPS)):
        adjoint = advance_weights(adjoint, weight_pad[0, step], weight_pad[1, step], staying)
        gradient = gradient + adjoint * tracer[step]
    highest = lax.Precision.HIGHEST
    y_lines = lax.all_to_all(gradient, "gy", split_axis=1, concat_axis=2, tiled=True)
    x_share = y_lines.shape[1]
    full_y = y_lines.shape[2]
    line_count = y_lines.shape[0] * x_share
    smooth_y = lax.dot_general(
        correlation(full_y, 2 * brick_y),
        y_lines.reshape(line_count, full_y),
        (((1,), (1,)), ((), ())),
        precision=highest,
        preferred_element_type=jnp.float32,
    )
    planes = lax.all_to_all(
        lax.all_to_all(smooth_y, ("gx", "gy"), split_axis=0, concat_axis=1, tiled=True),
        "gz",
        split_axis=0,
        concat_axis=1,
        tiled=True,
    )
    y_rows = planes.shape[0]
    depth_groups = lax.axis_size("gz")
    plane_view = planes.reshape(y_rows, depth_groups, groups, brick_z, x_share)
    full_x = groups * x_share
    table_x = correlation(full_x, 2 * brick_x).reshape(full_x, groups, x_share)
    smooth_x = jnp.einsum("ykdza,jda->ykzj", plane_view, table_x, precision=highest)
    full_z = depth_groups * brick_z
    smooth_x = smooth_x.reshape(y_rows, full_z, full_x)
    smoothed = jnp.einsum(
        "yzj,iz->yij", smooth_x, correlation(full_z, 2 * brick_z), precision=highest
    )
    return (adjoint, smoothed)


def solution(mesh):
    return jax.shard_map(
        per_device,
        mesh=mesh,
        in_specs=(
            P(("gx", "gy"), "gz"),
            P(("gx", "gy"), None),
            P(("gx", "gy")),
            P(None, "gz", "gx", "gy"),
            P(None, "gz", "gx", "gy"),
            P(None, "gz", "gx", "gy"),
        ),
        out_specs=(P("gz", "gx", "gy"), P(("gx", "gy", "gz"), None, None)),
        check_vma=False,
    )
```

profile of v0, /device:TPU:1, one launch (start us, length us, event | category | flops | bytes accessed | tf_op | source)
XLA Modules:
  0.0 618.9 jit_solution(1753815041108908470)
XLA Ops:
  12.2 1.4 copy.58
  13.6 2.7 fusion.12
  17.0 1.4 copy-done
  19.3 4.0 collective-permute-start
  23.3 1.3 collective-permute-start.1
  24.7 4.7 collective-permute-done
  29.3 3.9 collective-permute-done.1
  33.3 2.7 pad_maximum_fusion.1
  35.9 6.3 %fusion.95 = (f32[2,3,3,32,18,1]{5,3,4,2,1,0:T(8,128)}, f32[2,3,3,32,18,1]{5,3,4,2,1,0:T(8,128)}) fusion(f32[2,3,3,32,18,128]{5,3,4,2,1,0:T(8,128)S(1)} %pad_maximum_fusion.1), kind=kLoop, calls=%fused_computation.232 | loop fusion | bytes 165888 | tf_op jit(solution)/shard_map/slice | solution.py:16
  42.2 3.9 copy.71
  46.1 3.5 collective-permute-start.2
  49.7 4.4 copy.72
  55.4 172.0 %all-reduce.5.cloned.1.call-done = (s32[12288]{0:T(1024)}, s32[12288]{0:T(1024)}) async-done(((s32[12288]{0:T(1024)}, s32[12288]{0:T(1024)}), (s32[12288]{0:T(1024)}, s32[12288]{0:T(1024)})) %all-reduce.5.cloned.1.call-update) | async-done | bytes 98320
  228.2 3.6 copy.73
  231.8 4.5 copy.74
  236.2 107.2 %all-gather.4.cloned.1.call-done = f32[128,96,32]{1,2,0:T(8,128)} async-done(((f32[1,96,32]{1,2,0:T(8,128)}), f32[128,96,32]{1,2,0:T(8,128)}) %all-gather.4.cloned.1.call-update) | async-done | bytes 1572880 | tf_op jit(solution)/shard_map/all_gather | solution.py:57
  343.4 5.3 copy.90
  348.7 67.0 %scatter_custom_fusion = f32[32,2048]{0,1:T(8,128)} fusion(s32[12288]{0:T(1024)S(1)} %compare_select_fusion, f32[12288,32]{1,0:T(8,128)} %bitcast.160, f32[]{:T(128)} %constant.79.clone.1), kind=kCustom, calls=%fused_computation.47 | custom fusion | flops 393216 | bytes 262656 | tf_op jit(solution)/shard_map/scatter-add | solution.py:65
  415.7 1.5 copy.63
  418.6 4.6 collective-permute-start.7
  423.1 6.4 %pad_maximum_fusion.7 = (f32[2,3,3,1,18,130]{5,3,4,2,1,0:T(1,128)S(1)}, f32[2,3,3,1,18,130]{5,3,4,2,1,0:T(1,128)S(1)}) fusion(f32[2,3,3,32,18,1]{5,3,4,2,1,0:T(8,128)} %copy.74, f32[2,3,3,32,18,1]{5,3,4,2,1,0:T(8,128)} %copy.73, f32[2,3,3,32,1,128]{5,3,4,2,1,0:T(8,128)} %collective-permute-done.1, f32[2,3,3,32,1,128]{5,3,4,2,1,0:T(8,128)} %copy-done.2, ...), kind=kLoop, calls=%fused_computation.55 | loop fusion | flops 421200 | bytes 5728320 | tf_op jit(solution)/shard_map/slice | solution.py:16
  430.9 8.1 %collective-permute-start.5 = (f32[2,3,3,1,18,130]{5,3,4,2,1,0:T(1,128)S(1)}, f32[2,3,3,1,18,130]{5,3,4,2,1,0:T(1,128)S(1)}, u32[]{:S(2)}, u32[]{:S(2)}) collective-permute-start(f32[2,3,3,1,18,130]{5,3,4,2,1,0:T(1,128)S(1)} %get-tuple-element.13), channel_id=1, source_target_pairs={{1,0},{3,2},{5,4},{7,6},{9,8},{11,10},{13,12},{15,14},{17,16},{19,... | collective-permute-start | bytes 505448 | tf_op jit(solution)/shard_map/ppermute | solution.py:18
  440.5 4.0 collective-permute-start.9
  444.6 17.7 %pad_maximum_fusion = f32[2,3,3,34,18,130]{5,3,4,2,1,0:T(8,128)} fusion(f32[2,3,3,1,18,130]{5,3,4,2,1,0:T(1,128)S(1)} %collective-permute-done.5, f32[2,3,3,32,18,1]{5,3,4,2,1,0:T(8,128)S(1)} %bitcast.158, f32[2,3,3,32,1,128]{5,3,4,2,1,0:T(8,128)} %collective-permute-done.1, f32[1,3,3,32,16,128]{5,3,4,2,1,0:T(8,128)S(1)} %copy-done.1, ...), kind=kLoop, calls=%fused_computation.1 | loop fusion | flops 10024560 | bytes 11456640 | tf_op jit(solution)/shard_map/concatenate | solution.py:19
  462.5 1.8 collective-permute-start.10
  465.6 9.0 %slice_bitcast_fusion.1 = (f32[3,34,18,130]{3,1,2,0:T(8,128)S(1)}, f32[3,34,18,130]{3,1,2,0:T(8,128)}, f32[3,34,18,130]{3,1,2,0:T(8,128)}, f32[3,34,18,130]{3,1,...) fusion(f32[2,3,3,34,18,130]{5,3,4,2,1,0:T(8,128)} %pad_maximum_fusion), kind=kLoop, calls=%fused_computation.13 | loop fusion | bytes 11456640 | tf_op jit(solution)/shard_map/squeeze | solution.py:76
  474.7 3.1 fusion.47
  479.1 4.1 collective-permute-start.13
  485.5 4.0 collective-permute-start.15
  489.5 2.9 collective-permute-done.14
  493.4 5.5 collective-permute-start.16
  500.1 1.8 collective-permute-done.17
  501.9 2.8 fusion.35
  504.7 1.3 collective-permute-start.18
  506.0 4.4 collective-permute-start.19
  512.7 4.8 collective-permute-start.21
  517.5 4.4 collective-permute-done.20
  523.0 3.8 collective-permute-start.22
  528.1 1.7 collective-permute-done.23
  529.8 2.9 fusion.61
  532.7 9.9 %all-to-all-start = ((f32[32,16,128]{2,0,1:T(8,128)}), f32[32,16,128]{2,0,1:T(8,128)S(1)}, u32[]{:S(2)}, u32[]{:S(2)}) async-start(f32[32,16,128]{2,0,1:T(8,128)} %get-tuple-element.8), calls=%async_computation | async-start | bytes 524288 | tf_op jit(solution)/shard_map/all_to_all | solution.py:79
  542.6 12.2 %all-to-all-done = f32[32,16,128]{2,0,1:T(8,128)S(1)} async-done(((f32[32,16,128]{2,0,1:T(8,128)}), f32[32,16,128]{2,0,1:T(8,128)S(1)}, u32[]{:S(2)}, u32[]{:S(2)}) %all-to-all-start) | async-done | bytes 262176 | tf_op jit(solution)/shard_map/all_to_all | solution.py:79
  555.1 5.0 fusion
  561.3 14.9 %all-to-all-start.1 = ((f32[128,1,512]{2,1,0:T(1,128)}), f32[128,1,512]{2,1,0:T(1,128)S(1)}, u32[]{:S(2)}, u32[]{:S(2)}) async-start(f32[128,1,512]{2,1,0:T(1,128)} %reshape.198), calls=%async_computation.1 | async-start | bytes 524288 | tf_op jit(solution)/shard_map/all_to_all | solution.py:91
  577.1 13.1 %all-to-all-done.1 = f32[128,1,512]{2,1,0:T(1,128)S(1)} async-done(((f32[128,1,512]{2,1,0:T(1,128)}), f32[128,1,512]{2,1,0:T(1,128)S(1)}, u32[]{:S(2)}, u32[]{:S(2)}) %all-to-all-start.1) | async-done | bytes 262176 | tf_op jit(solution)/shard_map/all_to_all | solution.py:91
  592.5 5.6 all_to_all.44
  598.1 5.1 copy.86
  603.2 7.2 %copy.87 = f32[4,2,32,2,128]{4,2,1,3,0:T(8,128)S(1)} copy(f32[4,2,32,2,128]{0,3,2,4,1:T(2,128)} %bitcast.159) | data formatting | bytes 524288 | tf_op jit(solution)/shard_map/ykdza,jda->ykzj/dot_general | solution.py:102
  (97 shorter events, 30.4 us)
Async XLA Ops:
  7.2 220.2 %all-reduce.5.cloned.1.call-start = ((), (), s32[]{:S(2)}) async-start(), calls=%async_computation.4 | async-start | bytes 196608
  9.9 0.9 copy-start.8
  10.8 0.6 copy-start.7
  11.5 331.9 %all-gather.4.cloned.1.call-start = ((), (), s32[]{:S(2)}) async-start(), calls=%async_computation.3 | async-start | bytes 2113536 | tf_op jit(solution)/shard_map/all_gather | solution.py:57
  17.0 1.4 copy-start
  19.3 10.0 %collective-permute-start = (f32[2,3,3,32,1,128]{5,3,4,2,1,0:T(8,128)}, f32[2,3,3,32,1,128]{5,3,4,2,1,0:T(8,128)S(1)}, u32[]{:S(2)}, u32[]{:S(2)}) collective-permute-start(f32[2,3,3,32,1,128]{5,3,4,2,1,0:T(8,128)} %get-tuple-element.22), channel_id=1, source_target_pairs={{0,16},{16,32},{32,48},{48,64},{64,80},{80,96},{96,112},{112,128},... | collective-permute-start | bytes 884744 | tf_op jit(solution)/shard_map/ppermute | solution.py:15
  23.3 9.9 %collective-permute-start.1 = (f32[2,3,3,32,1,128]{5,3,4,2,1,0:T(8,128)}, f32[2,3,3,32,1,128]{5,3,4,2,1,0:T(8,128)}, u32[]{:S(2)}, u32[]{:S(2)}) collective-permute-start(f32[2,3,3,32,1,128]{5,3,4,2,1,0:T(8,128)} %get-tuple-element.23), channel_id=1, source_target_pairs={{16,0},{32,16},{48,32},{64,48},{80,64},{96,80},{112,96},{128,112},... | collective-permute-start | bytes 884744 | tf_op jit(solution)/shard_map/ppermute | solution.py:18
  29.3 6.6 %copy-start.2 = (f32[2,3,3,32,1,128]{5,3,4,2,1,0:T(8,128)}, f32[2,3,3,32,1,128]{5,3,4,2,1,0:T(8,128)S(1)}, u32[]{:S(2)}) copy-start(f32[2,3,3,32,1,128]{5,3,4,2,1,0:T(8,128)S(1)} %collective-permute-done) | copy-start | bytes 884740
  46.1 182.1 %collective-permute-start.2 = (f32[2,3,3,32,18,1]{3,0,5,4,2,1:T(2,128)S(1)}, f32[2,3,3,32,18,1]{3,0,5,4,2,1:T(2,128)S(1)}, u32[]{:S(2)}, u32[]{:S(2)}) collective-permute-start(f32[2,3,3,32,18,1]{3,0,5,4,2,1:T(2,128)S(1)} %copy.71), channel_id=1, source_target_pairs={{0,2},{2,4},{4,6},{6,8},{8,10},{10,12},{12,14},{1,3},{3,5},{5,7},{... | collective-permute-start | bytes 124424 | tf_op jit(solution)/shard_map/ppermute | solution.py:15
  54.1 177.7 %collective-permute-start.3 = (f32[2,3,3,32,18,1]{3,0,5,4,2,1:T(2,128)}, f32[2,3,3,32,18,1]{3,0,5,4,2,1:T(2,128)}, u32[]{:S(2)}, u32[]{:S(2)}) collective-permute-start(f32[2,3,3,32,18,1]{3,0,5,4,2,1:T(2,128)} %copy.72), channel_id=1, source_target_pairs={{2,0},{4,2},{6,4},{8,6},{10,8},{12,10},{14,12},{3,1},{5,3},{7,5},{... | collective-permute-start | bytes 124424 | tf_op jit(solution)/shard_map/ppermute | solution.py:18
  417.2 21.8 %collective-permute-start.6 = (f32[32,1,128]{2,0,1:T(8,128)S(1)}, f32[32,1,128]{2,0,1:T(8,128)S(1)}, u32[]{:S(2)}, u32[]{:S(2)}) collective-permute-start(f32[32,1,128]{2,0,1:T(8,128)S(1)} %get-tuple-element.49), channel_id=1, source_target_pairs={{16,0},{32,16},{48,32},{64,48},{80,64},{96,80},{112,96},{128,112},... | collective-permute-start | bytes 49160 | tf_op jit(solution)/shard_map/ppermute | solution.py:18
  418.5 26.0 %slice-start = ((s8[5308416]{0:T(1024)(128)(4,1)}), s8[4194304]{0:T(1024)(128)(4,1)S(1)}, s32[]{:S(2)}) async-start(s8[5308416]{0:T(1024)(128)(4,1)} %bitcast.155), calls=%async_computation.5 | async-start | bytes 8388608
  418.5 26.0 %slice-start.2 = ((s8[5308416]{0:T(1024)(128)(4,1)}), s8[4194304]{0:T(1024)(128)(4,1)S(1)}, s32[]{:S(2)}) async-start(s8[5308416]{0:T(1024)(128)(4,1)} %bitcast.157), calls=%async_computation.7 | async-start | bytes 8388608
  418.5 26.0 %copy-start.1 = (f32[1,3,3,32,16,128]{5,3,4,2,1,0:T(8,128)S(1)}, f32[1,3,3,32,16,128]{5,3,4,2,1,0:T(8,128)}, u32[]{:S(2)}) copy-start(f32[1,3,3,32,16,128]{5,3,4,2,1,0:T(8,128)} %copy-done) | copy-start | bytes 7077892
  418.5 26.0 %slice-start.1 = ((s8[5308416]{0:T(1024)(128)(4,1)}), s8[1114112]{0:T(1024)(128)(4,1)S(1)}, s32[]{:S(2)}) async-start(s8[5308416]{0:T(1024)(128)(4,1)} %bitcast.155), calls=%async_computation.6 | async-start | bytes 2228224
  418.6 26.0 %slice-start.3 = ((s8[5308416]{0:T(1024)(128)(4,1)}), s8[1114112]{0:T(1024)(128)(4,1)S(1)}, s32[]{:S(2)}) async-start(s8[5308416]{0:T(1024)(128)(4,1)} %bitcast.157), calls=%async_computation.8 | async-start | bytes 2228224
  418.6 26.0 %copy-start.3 = (f32[2,3,3,32,1,128]{5,3,4,2,1,0:T(8,128)S(1)}, f32[2,3,3,32,1,128]{5,3,4,2,1,0:T(8,128)}, u32[]{:S(2)}) copy-start(f32[2,3,3,32,1,128]{5,3,4,2,1,0:T(8,128)} %copy-done.2) | copy-start | bytes 884740
  418.6 20.4 %collective-permute-start.7 = (f32[32,1,128]{2,0,1:T(8,128)S(1)}, f32[32,1,128]{2,0,1:T(8,128)S(1)}, u32[]{:S(2)}, u32[]{:S(2)}) collective-permute-start(f32[32,1,128]{2,0,1:T(8,128)S(1)} %get-tuple-element.48), channel_id=1, source_target_pairs={{0,16},{16,32},{32,48},{48,64},{64,80},{80,96},{96,112},{112,128},... | collective-permute-start | bytes 49160 | tf_op jit(solution)/shard_map/ppermute | solution.py:15
  429.6 14.9 %collective-permute-start.4 = (f32[2,3,3,1,18,130]{5,3,4,2,1,0:T(1,128)S(1)}, f32[2,3,3,1,18,130]{5,3,4,2,1,0:T(1,128)S(1)}, u32[]{:S(2)}, u32[]{:S(2)}) collective-permute-start(f32[2,3,3,1,18,130]{5,3,4,2,1,0:T(1,128)S(1)} %get-tuple-element.12), channel_id=1, source_target_pairs={{0,1},{2,3},{4,5},{6,7},{8,9},{10,11},{12,13},{14,15},{16,17},{18,... | collective-permute-start | bytes 505448 | tf_op jit(solution)/shard_map/ppermute | solution.py:15
  430.9 13.6 %collective-permute-start.5 = (f32[2,3,3,1,18,130]{5,3,4,2,1,0:T(1,128)S(1)}, f32[2,3,3,1,18,130]{5,3,4,2,1,0:T(1,128)S(1)}, u32[]{:S(2)}, u32[]{:S(2)}) collective-permute-start(f32[2,3,3,1,18,130]{5,3,4,2,1,0:T(1,128)S(1)} %get-tuple-element.13), channel_id=1, source_target_pairs={{1,0},{3,2},{5,4},{7,6},{9,8},{11,10},{13,12},{15,14},{17,16},{19,... | collective-permute-start | bytes 505448 | tf_op jit(solution)/shard_map/ppermute | solution.py:18
  439.2 23.1 %collective-permute-start.8 = (f32[32,18,1]{2,0,1:T(8,128)S(1)}, f32[32,18,1]{2,0,1:T(8,128)S(1)}, u32[]{:S(2)}, u32[]{:S(2)}) collective-permute-start(f32[32,18,1]{2,0,1:T(8,128)S(1)} %get-tuple-element.43), channel_id=1, source_target_pairs={{2,0},{4,2},{6,4},{8,6},{10,8},{12,10},{14,12},{3,1},{5,3},{7,5},{... | collective-permute-start | bytes 6920 | tf_op jit(solution)/shard_map/ppermute | solution.py:18
  440.5 21.8 %collective-permute-start.9 = (f32[32,18,1]{2,0,1:T(8,128)S(1)}, f32[32,18,1]{2,0,1:T(8,128)S(1)}, u32[]{:S(2)}, u32[]{:S(2)}) collective-permute-start(f32[32,18,1]{2,0,1:T(8,128)S(1)} %get-tuple-element.42), channel_id=1, source_target_pairs={{0,2},{2,4},{4,6},{6,8},{8,10},{10,12},{12,14},{1,3},{3,5},{5,7},{... | collective-permute-start | bytes 6920 | tf_op jit(solution)/shard_map/ppermute | solution.py:15
  462.3 2.0 copy-start.4
  462.3 2.0 copy-start.5
  462.5 12.2 %collective-permute-start.10 = (f32[1,18,130]{2,0,1:T(1,128)S(1)}, f32[1,18,130]{2,0,1:T(1,128)S(1)}, u32[]{:S(2)}, u32[]{:S(2)}) collective-permute-start(f32[1,18,130]{2,0,1:T(1,128)S(1)} %get-tuple-element.30), channel_id=1, source_target_pairs={{1,0},{3,2},{5,4},{7,6},{9,8},{11,10},{13,12},{15,14},{17,16},{19,... | collective-permute-start | bytes 28088 | tf_op jit(solution)/shard_map/ppermute | solution.py:18
  464.3 10.3 %collective-permute-start.11 = (f32[1,18,130]{2,0,1:T(1,128)S(1)}, f32[1,18,130]{2,0,1:T(1,128)S(1)}, u32[]{:S(2)}, u32[]{:S(2)}) collective-permute-start(f32[1,18,130]{2,0,1:T(1,128)S(1)} %get-tuple-element.31), channel_id=1, source_target_pairs={{0,1},{2,3},{4,5},{6,7},{8,9},{10,11},{12,13},{14,15},{16,17},{18,... | collective-permute-start | bytes 28088 | tf_op jit(solution)/shard_map/ppermute | solution.py:15
  477.8 5.4 collective-permute-start.12
  479.1 49.0 %copy-start.6 = (f32[3,32,16,128]{3,2,1,0:T(8,128)S(1)}, f32[3,32,16,128]{3,2,1,0:T(8,128)}, u32[]{:S(2)}) copy-start(f32[3,32,16,128]{3,2,1,0:T(8,128)} %param.11) | copy-start | bytes 2359300
  479.1 5.0 collective-permute-start.13
  484.2 8.2 %collective-permute-start.14 = (f32[32,18,1]{2,0,1:T(8,128)S(1)}, f32[32,18,1]{2,0,1:T(8,128)S(1)}, u32[]{:S(2)}, u32[]{:S(2)}) collective-permute-start(f32[32,18,1]{2,0,1:T(8,128)S(1)} %get-tuple-element.41), channel_id=1, source_target_pairs={{2,0},{4,2},{6,4},{8,6},{10,8},{12,10},{14,12},{3,1},{5,3},{7,5},{... | collective-permute-start | bytes 6920 | tf_op jit(solution)/shard_map/ppermute | solution.py:18
  485.5 7.6 %collective-permute-start.15 = (f32[32,18,1]{2,0,1:T(8,128)S(1)}, f32[32,18,1]{2,0,1:T(8,128)S(1)}, u32[]{:S(2)}, u32[]{:S(2)}) collective-permute-start(f32[32,18,1]{2,0,1:T(8,128)S(1)} %get-tuple-element.40), channel_id=1, source_target_pairs={{0,2},{2,4},{4,6},{6,8},{8,10},{10,12},{12,14},{1,3},{3,5},{5,7},{... | collective-permute-start | bytes 6920 | tf_op jit(solution)/shard_map/ppermute | solution.py:15
  493.4 6.8 %collective-permute-start.16 = (f32[1,18,130]{2,0,1:T(1,128)S(1)}, f32[1,18,130]{2,0,1:T(1,128)S(1)}, u32[]{:S(2)}, u32[]{:S(2)}) collective-permute-start(f32[1,18,130]{2,0,1:T(1,128)S(1)} %get-tuple-element.28), channel_id=1, source_target_pairs={{1,0},{3,2},{5,4},{7,6},{9,8},{11,10},{13,12},{15,14},{17,16},{19,... | collective-permute-start | bytes 28088 | tf_op jit(solution)/shard_map/ppermute | solution.py:18
  498.8 3.1 collective-permute-start.17
  504.7 5.7 collective-permute-start.18
  506.0 5.2 collective-permute-start.19
  511.4 10.5 %collective-permute-start.20 = (f32[32,18,1]{2,0,1:T(8,128)S(1)}, f32[32,18,1]{2,0,1:T(8,128)S(1)}, u32[]{:S(2)}, u32[]{:S(2)}) collective-permute-start(f32[32,18,1]{2,0,1:T(8,128)S(1)} %get-tuple-element.39), channel_id=1, source_target_pairs={{2,0},{4,2},{6,4},{8,6},{10,8},{12,10},{14,12},{3,1},{5,3},{7,5},{... | collective-permute-start | bytes 6920 | tf_op jit(solution)/shard_map/ppermute | solution.py:18
  512.7 10.1 %collective-permute-start.21 = (f32[32,18,1]{2,0,1:T(8,128)S(1)}, f32[32,18,1]{2,0,1:T(8,128)S(1)}, u32[]{:S(2)}, u32[]{:S(2)}) collective-permute-start(f32[32,18,1]{2,0,1:T(8,128)S(1)} %get-tuple-element.38), channel_id=1, source_target_pairs={{0,2},{2,4},{4,6},{6,8},{8,10},{10,12},{12,14},{1,3},{3,5},{5,7},{... | collective-permute-start | bytes 6920 | tf_op jit(solution)/shard_map/ppermute | solution.py:15
  523.0 5.2 collective-permute-start.22
  526.7 3.1 collective-permute-start.23
  532.7 22.2 %all-to-all-start = ((f32[32,16,128]{2,0,1:T(8,128)}), f32[32,16,128]{2,0,1:T(8,128)S(1)}, u32[]{:S(2)}, u32[]{:S(2)}) async-start(f32[32,16,128]{2,0,1:T(8,128)} %get-tuple-element.8), calls=%async_computation | async-start | bytes 524288 | tf_op jit(solution)/shard_map/all_to_all | solution.py:79
  561.3 28.9 %all-to-all-start.1 = ((f32[128,1,512]{2,1,0:T(1,128)}), f32[128,1,512]{2,1,0:T(1,128)S(1)}, u32[]{:S(2)}, u32[]{:S(2)}) async-start(f32[128,1,512]{2,1,0:T(1,128)} %reshape.198), calls=%async_computation.1 | async-start | bytes 524288 | tf_op jit(solution)/shard_map/all_to_all | solution.py:91
Sparse Core Ops, SparseCore 0:
  14.1 213.2 all-reduce.4
  231.1 112.2 all-gather.3
where the time goes:
time: 620 us; the launch traced here: 619 us
  waiting for transfers between devices  328 us (53%)
  other arithmetic  109 us (18%)
  starting transfers between devices  92.9 us (15%)
  local copies, waits for them, and re-layouts  61 us (10%)
  between operations  15.4 us (2%)
  matrix products  6.64 us (1%)
    unnamed x3, waiting for transfers between devices  173 us
    all_gather x1, waiting for transfers between devices, per_device(): lax.all_gather(well_sources, ('gx', 'gy'), axis=0, tiled=True)  107 us
    scatter-add x1, other arithmetic, per_device(): landed = jnp.zeros((brick_z, columns), jnp.float32).at[:, target].add(jnp...  67 us
    ppermute x12, starting transfers between devices, with_halo(): lax.ppermute(lax.slice_in_dim(block, block.shape[dim] - width, None, axis...  38.6 us
    ppermute x12, starting transfers between devices, with_halo(): lax.ppermute(lax.slice_in_dim(block, 0, width, axis=dim), axis, backward)  29.5 us
    concatenate x5, other arithmetic, with_halo(): block = jnp.concatenate([low, block, high], axis=dim)  20.4 us
    all_to_all x1, starting transfers between devices, per_device(): lax.all_to_all(smooth_y, ('gx', 'gy'), split_axis=0, concat_axis=1, tiled...  14.9 us
    unnamed x36, local copies, waits for them, and re-layouts  13.7 us
  transfers between devices with their start and end apart: 28, of which 14 were waited for; matrix products, arithmetic and copies ran while one was open for 11% of the time, Pallas kernels for 0%

commit v1 on v0

--- a/solution.py
+++ b/solution.py
@@ -5,6 +5,13 @@
 from jax.sharding import PartitionSpec as P
 
 STEPS = 3
+
+
+def gather_over(block, name, dim):
+    size = lax.axis_size(name)
+    blocks = jnp.stack([block for _ in range(size)])
+    blocks = lax.all_to_all(blocks, name, split_axis=0, concat_axis=0)
+    return jnp.concatenate(blocks, axis=dim)
 
 
 def with_halo(block, sides, width):
@@ -54,7 +61,7 @@
     my_owner = lax.axis_index("gx") * lax.axis_size("gy") + lax.axis_index("gy")
     owners = well_owner[:, 0]
     all_sources, all_owner, all_cell = (
-        lax.all_gather(well_sources, ("gx", "gy"), axis=0, tiled=True),
+        gather_over(well_sources, ("gx", "gy"), 0),
         lax.all_gather(owners, ("gx", "gy"), axis=0, tiled=True),
         lax.all_gather(well_cell, ("gx", "gy"), axis=0, tiled=True),
     )

time: 620 us -> 536 us (0.86)
  waiting for transfers between devices: 328 us -> 232 us
  starting transfers between devices: 92.9 us -> 107 us
    all_gather x1 -> x0, waiting for transfers between devices: 107 us -> none  [per_device(): lax.all_gather(well_sources, ('gx', 'gy'), axis=0, tiled=True)]
    all_to_all x0 -> x1, starting transfers between devices: none -> 16.9 us  [gather_over(): blocks = lax.all_to_all(blocks, name, split_axis=0, concat_axis=0)]
    unnamed x3 -> x2, waiting for transfers between devices: 173 us -> 182 us
    unnamed x36 -> x45, local copies, waits for them, and re-layouts: 13.7 us -> 5.31 us
  transfers between devices with their start and end apart: 28 -> 28, of which waited for: 14 -> 13; matrix products, arithmetic and copies ran while one was open for 11% -> 12% of each run, Pallas kernels for 0% -> 0%
where the time goes in v1:
time: 536 us; the launch traced here: 535 us
  waiting for transfers between devices  232 us (43%)
  other arithmetic  108 us (20%)
  starting transfers between devices  107 us (20%)
  local copies, waits for them, and re-layouts  60.2 us (11%)
  between operations  15.5 us (3%)
  matrix products  6.64 us (1%)
  blocking collectives  5.63 us (1%)
    unnamed x2, waiting for transfers between devices  182 us
    scatter-add x1, other arithmetic, per_device(): landed = jnp.zeros((brick_z, columns), jnp.float32).at[:, target].add(jnp...  66.9 us
    ppermute x12, starting transfers between devices, with_halo(): lax.ppermute(lax.slice_in_dim(block, block.shape[dim] - width, None, axis...  36 us
    ppermute x12, starting transfers between devices, with_halo(): lax.ppermute(lax.slice_in_dim(block, 0, width, axis=dim), axis, backward)  29.2 us
    concatenate x5, other arithmetic, with_halo(): block = jnp.concatenate([low, block, high], axis=dim)  20.4 us
    all_to_all x1, starting transfers between devices, gather_over(): blocks = lax.all_to_all(blocks, name, split_axis=0, concat_axis=0)  16.9 us
    all_to_all x1, starting transfers between devices, per_device(): lax.all_to_all(smooth_y, ('gx', 'gy'), split_axis=0, concat_axis=1, tiled...  15.5 us
    ppermute x12, waiting for transfers between devices, with_halo(): lax.ppermute(lax.slice_in_dim(block, block.shape[dim] - width, None, axis...  15 us
  transfers between devices with their start and end apart: 28, of which 13 were waited for; matrix products, arithmetic and copies ran while one was open for 12% of the time, Pallas kernels for 0%

profile of v1, /device:TPU:1, one launch (start us, length us, event | category | flops | bytes accessed | tf_op | source)
XLA Modules:
  0.0 534.9 jit_solution(2173741415683931061)
XLA Ops:
  7.2 2.4 stack.12
  9.6 16.9 %all-to-all-start = ((f32[128,96,32]{1,2,0:T(8,128)}), f32[128,96,32]{1,2,0:T(8,128)}, u32[]{:S(2)}, u32[]{:S(2)}) async-start(f32[128,96,32]{1,2,0:T(8,128)} %stack.12), calls=%async_computation | async-start | bytes 4194304 | tf_op jit(solution)/shard_map/all_to_all | solution.py:13
  26.8 1.6 fusion.12
  29.1 1.3 copy-done
  31.4 2.4 collective-permute-start
  37.4 8.2 %collective-permute-done = f32[2,3,3,32,1,128]{5,3,4,2,1,0:T(8,128)S(1)} collective-permute-done((f32[2,3,3,32,1,128]{5,3,4,2,1,0:T(8,128)}, f32[2,3,3,32,1,128]{5,3,4,2,1,0:T(8,128)S(1)}, u32[]{:S(2)}, u32[]{:S(2)}) %collective-permute-start) | collective-permute-done | bytes 294944 | tf_op jit(solution)/shard_map/ppermute | solution.py:22
  45.6 2.8 collective-permute-done.1
  48.4 2.6 pad_maximum_fusion.1
  51.0 6.3 %fusion.95 = (f32[2,3,3,32,18,1]{5,3,4,2,1,0:T(8,128)}, f32[2,3,3,32,18,1]{5,3,4,2,1,0:T(8,128)}) fusion(f32[2,3,3,32,18,128]{5,3,4,2,1,0:T(8,128)S(1)} %pad_maximum_fusion.1), kind=kLoop, calls=%fused_computation.232 | loop fusion | bytes 165888 | tf_op jit(solution)/shard_map/slice | solution.py:23
  57.3 3.9 copy.69
  61.1 2.5 collective-permute-start.2
  63.6 4.4 copy.70
  68.0 1.5 collective-permute-start.3
  69.5 181.7 %all-reduce.5.cloned.1.call-done = (s32[12288]{0:T(1024)}, s32[12288]{0:T(1024)}) async-done(((s32[12288]{0:T(1024)}, s32[12288]{0:T(1024)}), (s32[12288]{0:T(1024)}, s32[12288]{0:T(1024)})) %all-reduce.5.cloned.1.call-update) | async-done | bytes 98320
  252.1 3.6 copy.71
  255.7 4.4 copy.72
  260.1 5.3 copy.88
  265.5 66.9 %scatter_custom_fusion = f32[32,2048]{0,1:T(8,128)} fusion(s32[12288]{0:T(1024)S(1)} %compare_select_fusion, f32[12288,32]{1,0:T(8,128)} %bitcast.159, f32[]{:T(128)} %constant.79.clone.1), kind=kCustom, calls=%fused_computation.47 | custom fusion | flops 393216 | bytes 262656 | tf_op jit(solution)/shard_map/scatter-add | solution.py:72
  332.4 1.5 copy.61
  335.3 4.5 collective-permute-start.7
  339.8 6.5 %pad_maximum_fusion.7 = (f32[2,3,3,1,18,130]{5,3,4,2,1,0:T(1,128)S(1)}, f32[2,3,3,1,18,130]{5,3,4,2,1,0:T(1,128)S(1)}) fusion(f32[2,3,3,32,18,1]{5,3,4,2,1,0:T(8,128)} %copy.72, f32[2,3,3,32,18,1]{5,3,4,2,1,0:T(8,128)} %copy.71, f32[2,3,3,32,1,128]{5,3,4,2,1,0:T(8,128)} %collective-permute-done.1, f32[2,3,3,32,1,128]{5,3,4,2,1,0:T(8,128)} %copy-done.2, ...), kind=kLoop, calls=%fused_computation.55 | loop fusion | flops 421200 | bytes 5728320 | tf_op jit(solution)/shard_map/slice | solution.py:23
  347.6 7.6 %collective-permute-start.5 = (f32[2,3,3,1,18,130]{5,3,4,2,1,0:T(1,128)S(1)}, f32[2,3,3,1,18,130]{5,3,4,2,1,0:T(1,128)S(1)}, u32[]{:S(2)}, u32[]{:S(2)}) collective-permute-start(f32[2,3,3,1,18,130]{5,3,4,2,1,0:T(1,128)S(1)} %get-tuple-element.13), channel_id=1, source_target_pairs={{1,0},{3,2},{5,4},{7,6},{9,8},{11,10},{13,12},{15,14},{17,16},{19,... | collective-permute-start | bytes 505448 | tf_op jit(solution)/shard_map/ppermute | solution.py:25
  356.7 4.0 collective-permute-start.9
  360.8 17.7 %pad_maximum_fusion = f32[2,3,3,34,18,130]{5,3,4,2,1,0:T(8,128)} fusion(f32[2,3,3,1,18,130]{5,3,4,2,1,0:T(1,128)S(1)} %collective-permute-done.5, f32[2,3,3,32,18,1]{5,3,4,2,1,0:T(8,128)S(1)} %bitcast.157, f32[2,3,3,32,1,128]{5,3,4,2,1,0:T(8,128)} %collective-permute-done.1, f32[1,3,3,32,16,128]{5,3,4,2,1,0:T(8,128)S(1)} %copy-done.1, ...), kind=kLoop, calls=%fused_computation.1 | loop fusion | flops 10024560 | bytes 11456640 | tf_op jit(solution)/shard_map/concatenate | solution.py:26
  378.7 1.8 collective-permute-start.10
  380.6 1.5 collective-permute-start.11
  382.1 9.0 %slice_bitcast_fusion.1 = (f32[3,34,18,130]{3,1,2,0:T(8,128)S(1)}, f32[3,34,18,130]{3,1,2,0:T(8,128)}, f32[3,34,18,130]{3,1,2,0:T(8,128)}, f32[3,34,18,130]{3,1,...) fusion(f32[2,3,3,34,18,130]{5,3,4,2,1,0:T(8,128)} %pad_maximum_fusion), kind=kLoop, calls=%fused_computation.13 | loop fusion | bytes 11456640 | tf_op jit(solution)/shard_map/squeeze | solution.py:83
  391.1 3.1 fusion.47
  395.5 4.1 collective-permute-start.13
  402.0 4.0 collective-permute-start.15
  406.0 2.9 collective-permute-done.14
  409.8 5.5 %collective-permute-start.16 = (f32[1,18,130]{2,0,1:T(1,128)S(1)}, f32[1,18,130]{2,0,1:T(1,128)S(1)}, u32[]{:S(2)}, u32[]{:S(2)}) collective-permute-start(f32[1,18,130]{2,0,1:T(1,128)S(1)} %get-tuple-element.28), channel_id=1, source_target_pairs={{1,0},{3,2},{5,4},{7,6},{9,8},{11,10},{13,12},{15,14},{17,16},{19,... | collective-permute-start | bytes 28088 | tf_op jit(solution)/shard_map/ppermute | solution.py:25
  416.6 1.8 collective-permute-done.17
  418.3 2.8 fusion.35
  422.4 4.4 collective-permute-start.19
  429.1 4.8 collective-permute-start.21
  433.9 4.4 collective-permute-done.20
  439.4 3.8 collective-permute-start.22
  444.5 1.7 collective-permute-done.23
  446.2 2.9 fusion.61
  449.1 9.2 %all-to-all-start.1 = ((f32[32,16,128]{2,0,1:T(8,128)}), f32[32,16,128]{2,0,1:T(8,128)S(1)}, u32[]{:S(2)}, u32[]{:S(2)}) async-start(f32[32,16,128]{2,0,1:T(8,128)} %get-tuple-element.8), calls=%async_computation.1 | async-start | bytes 524288 | tf_op jit(solution)/shard_map/all_to_all | solution.py:86
  458.4 12.2 %all-to-all-done.1 = f32[32,16,128]{2,0,1:T(8,128)S(1)} async-done(((f32[32,16,128]{2,0,1:T(8,128)}), f32[32,16,128]{2,0,1:T(8,128)S(1)}, u32[]{:S(2)}, u32[]{:S(2)}) %all-to-all-start.1) | async-done | bytes 262176 | tf_op jit(solution)/shard_map/all_to_all | solution.py:86
  470.8 5.0 fusion
  477.1 15.5 %all-to-all-start.2 = ((f32[128,1,512]{2,1,0:T(1,128)}), f32[128,1,512]{2,1,0:T(1,128)S(1)}, u32[]{:S(2)}, u32[]{:S(2)}) async-start(f32[128,1,512]{2,1,0:T(1,128)} %reshape.202), calls=%async_computation.2 | async-start | bytes 524288 | tf_op jit(solution)/shard_map/all_to_all | solution.py:98
  493.5 12.8 %all-to-all-done.2 = f32[128,1,512]{2,1,0:T(1,128)S(1)} async-done(((f32[128,1,512]{2,1,0:T(1,128)}), f32[128,1,512]{2,1,0:T(1,128)S(1)}, u32[]{:S(2)}, u32[]{:S(2)}) %all-to-all-start.2) | async-done | bytes 262176 | tf_op jit(solution)/shard_map/all_to_all | solution.py:98
  508.6 5.6 %all_to_all.49 = f32[2,4,8192]{2,1,0:T(4,128)S(1)} all-to-all(f32[2,4,8192]{2,1,0:T(4,128)S(1)} %all_to_all.42), channel_id=1, replica_groups=mesh['gx'=16,'gy'=8,'gz'=2] {'gz'}, dimensions={0} | all-to-all | bytes 524288 | tf_op jit(solution)/shard_map/all_to_all | solution.py:97
  514.2 5.0 copy.84
  519.2 7.2 %copy.85 = f32[4,2,32,2,128]{4,2,1,3,0:T(8,128)S(1)} copy(f32[4,2,32,2,128]{0,3,2,4,1:T(2,128)} %bitcast.158) | data formatting | bytes 524288 | tf_op jit(solution)/shard_map/ykdza,jda->ykzj/dot_general | solution.py:109
  (107 shorter events, 28.0 us)
Async XLA Ops:
  7.2 19.4 %copy-start.6 = (f32[3,32,16,128]{3,2,1,0:T(8,128)S(1)}, f32[3,32,16,128]{3,2,1,0:T(8,128)}, u32[]{:S(2)}) copy-start(f32[3,32,16,128]{3,2,1,0:T(8,128)} %param.10) | copy-start | bytes 2359300
  7.2 19.6 %copy-start.8 = (s32[3,32,16,128]{3,2,1,0:T(8,128)S(1)}, s32[3,32,16,128]{3,2,1,0:T(8,128)}, u32[]{:S(2)}) copy-start(s32[3,32,16,128]{3,2,1,0:T(8,128)} %param.9) | copy-start | bytes 2359300
  9.6 250.5 %all-to-all-start = ((f32[128,96,32]{1,2,0:T(8,128)}), f32[128,96,32]{1,2,0:T(8,128)}, u32[]{:S(2)}, u32[]{:S(2)}) async-start(f32[128,96,32]{1,2,0:T(8,128)} %stack.12), calls=%async_computation | async-start | bytes 4194304 | tf_op jit(solution)/shard_map/all_to_all | solution.py:13
  26.5 224.8 %all-reduce.5.cloned.1.call-start = ((), (), s32[]{:S(2)}) async-start(), calls=%async_computation.4 | async-start | bytes 196608
  29.1 1.4 copy-start
  29.1 6.0 %copy-start.13 = (u32[256]{0:T(256)S(1)}, u32[256]{0:T(256)}, u32[]{:S(2)}) copy-start(u32[256]{0:T(256)} %constant.102) | copy-start | bytes 3076
  29.1 7.2 %copy-start.11 = (s32[96]{0:T(128)S(1)}, s32[96]{0:T(128)}, u32[]{:S(2)}) copy-start(s32[96]{0:T(128)} %param.8) | copy-start | bytes 1156
  29.1 7.5 %copy-start.12 = (s32[96,1]{0,1:T(1,128)S(1)}, s32[96,1]{0,1:T(1,128)}, u32[]{:S(2)}) copy-start(s32[96,1]{0,1:T(1,128)} %param.7) | copy-start | bytes 1156
  31.4 14.2 %collective-permute-start = (f32[2,3,3,32,1,128]{5,3,4,2,1,0:T(8,128)}, f32[2,3,3,32,1,128]{5,3,4,2,1,0:T(8,128)S(1)}, u32[]{:S(2)}, u32[]{:S(2)}) collective-permute-start(f32[2,3,3,32,1,128]{5,3,4,2,1,0:T(8,128)} %get-tuple-element.22), channel_id=1, source_target_pairs={{0,16},{16,32},{32,48},{48,64},{64,80},{80,96},{96,112},{112,128},... | collective-permute-start | bytes 884744 | tf_op jit(solution)/shard_map/ppermute | solution.py:22
  33.8 14.6 %collective-permute-start.1 = (f32[2,3,3,32,1,128]{5,3,4,2,1,0:T(8,128)}, f32[2,3,3,32,1,128]{5,3,4,2,1,0:T(8,128)}, u32[]{:S(2)}, u32[]{:S(2)}) collective-permute-start(f32[2,3,3,32,1,128]{5,3,4,2,1,0:T(8,128)} %get-tuple-element.23), channel_id=1, source_target_pairs={{16,0},{32,16},{48,32},{64,48},{80,64},{96,80},{112,96},{128,112},... | collective-permute-start | bytes 884744 | tf_op jit(solution)/shard_map/ppermute | solution.py:25
  36.6 0.6 copy-start.10
  36.8 0.6 copy-start.9
  45.6 5.4 %copy-start.2 = (f32[2,3,3,32,1,128]{5,3,4,2,1,0:T(8,128)}, f32[2,3,3,32,1,128]{5,3,4,2,1,0:T(8,128)S(1)}, u32[]{:S(2)}) copy-start(f32[2,3,3,32,1,128]{5,3,4,2,1,0:T(8,128)S(1)} %collective-permute-done) | copy-start | bytes 884740
  61.1 190.9 %collective-permute-start.2 = (f32[2,3,3,32,18,1]{3,0,5,4,2,1:T(2,128)S(1)}, f32[2,3,3,32,18,1]{3,0,5,4,2,1:T(2,128)S(1)}, u32[]{:S(2)}, u32[]{:S(2)}) collective-permute-start(f32[2,3,3,32,18,1]{3,0,5,4,2,1:T(2,128)S(1)} %copy.69), channel_id=1, source_target_pairs={{0,2},{2,4},{4,6},{6,8},{8,10},{10,12},{12,14},{1,3},{3,5},{5,7},{... | collective-permute-start | bytes 124424 | tf_op jit(solution)/shard_map/ppermute | solution.py:22
  68.0 187.7 %collective-permute-start.3 = (f32[2,3,3,32,18,1]{3,0,5,4,2,1:T(2,128)}, f32[2,3,3,32,18,1]{3,0,5,4,2,1:T(2,128)}, u32[]{:S(2)}, u32[]{:S(2)}) collective-permute-start(f32[2,3,3,32,18,1]{3,0,5,4,2,1:T(2,128)} %copy.70), channel_id=1, source_target_pairs={{2,0},{4,2},{6,4},{8,6},{10,8},{12,10},{14,12},{3,1},{5,3},{7,5},{... | collective-permute-start | bytes 124424 | tf_op jit(solution)/shard_map/ppermute | solution.py:25
  334.0 21.2 %collective-permute-start.6 = (f32[32,1,128]{2,0,1:T(8,128)S(1)}, f32[32,1,128]{2,0,1:T(8,128)S(1)}, u32[]{:S(2)}, u32[]{:S(2)}) collective-permute-start(f32[32,1,128]{2,0,1:T(8,128)S(1)} %get-tuple-element.49), channel_id=1, source_target_pairs={{16,0},{32,16},{48,32},{64,48},{80,64},{96,80},{112,96},{128,112},... | collective-permute-start | bytes 49160 | tf_op jit(solution)/shard_map/ppermute | solution.py:25
  335.3 25.5 %slice-start = ((s8[5308416]{0:T(1024)(128)(4,1)}), s8[4194304]{0:T(1024)(128)(4,1)S(1)}, s32[]{:S(2)}) async-start(s8[5308416]{0:T(1024)(128)(4,1)} %bitcast.154), calls=%async_computation.5 | async-start | bytes 8388608
  335.3 25.5 %slice-start.2 = ((s8[5308416]{0:T(1024)(128)(4,1)}), s8[4194304]{0:T(1024)(128)(4,1)S(1)}, s32[]{:S(2)}) async-start(s8[5308416]{0:T(1024)(128)(4,1)} %bitcast.156), calls=%async_computation.7 | async-start | bytes 8388608
  335.3 25.5 %copy-start.1 = (f32[1,3,3,32,16,128]{5,3,4,2,1,0:T(8,128)S(1)}, f32[1,3,3,32,16,128]{5,3,4,2,1,0:T(8,128)}, u32[]{:S(2)}) copy-start(f32[1,3,3,32,16,128]{5,3,4,2,1,0:T(8,128)} %copy-done) | copy-start | bytes 7077892
  335.3 25.5 %slice-start.1 = ((s8[5308416]{0:T(1024)(128)(4,1)}), s8[1114112]{0:T(1024)(128)(4,1)S(1)}, s32[]{:S(2)}) async-start(s8[5308416]{0:T(1024)(128)(4,1)} %bitcast.154), calls=%async_computation.6 | async-start | bytes 2228224
  335.3 25.5 %slice-start.3 = ((s8[5308416]{0:T(1024)(128)(4,1)}), s8[1114112]{0:T(1024)(128)(4,1)S(1)}, s32[]{:S(2)}) async-start(s8[5308416]{0:T(1024)(128)(4,1)} %bitcast.156), calls=%async_computation.8 | async-start | bytes 2228224
  335.3 25.5 %copy-start.3 = (f32[2,3,3,32,1,128]{5,3,4,2,1,0:T(8,128)S(1)}, f32[2,3,3,32,1,128]{5,3,4,2,1,0:T(8,128)}, u32[]{:S(2)}) copy-start(f32[2,3,3,32,1,128]{5,3,4,2,1,0:T(8,128)} %copy-done.2) | copy-start | bytes 884740
  335.3 19.9 %collective-permute-start.7 = (f32[32,1,128]{2,0,1:T(8,128)S(1)}, f32[32,1,128]{2,0,1:T(8,128)S(1)}, u32[]{:S(2)}, u32[]{:S(2)}) collective-permute-start(f32[32,1,128]{2,0,1:T(8,128)S(1)} %get-tuple-element.48), channel_id=1, source_target_pairs={{0,16},{16,32},{32,48},{48,64},{64,80},{80,96},{96,112},{112,128},... | collective-permute-start | bytes 49160 | tf_op jit(solution)/shard_map/ppermute | solution.py:22
  346.3 14.4 %collective-permute-start.4 = (f32[2,3,3,1,18,130]{5,3,4,2,1,0:T(1,128)S(1)}, f32[2,3,3,1,18,130]{5,3,4,2,1,0:T(1,128)S(1)}, u32[]{:S(2)}, u32[]{:S(2)}) collective-permute-start(f32[2,3,3,1,18,130]{5,3,4,2,1,0:T(1,128)S(1)} %get-tuple-element.12), channel_id=1, source_target_pairs={{0,1},{2,3},{4,5},{6,7},{8,9},{10,11},{12,13},{14,15},{16,17},{18,... | collective-permute-start | bytes 505448 | tf_op jit(solution)/shard_map/ppermute | solution.py:22
  347.6 13.1 %collective-permute-start.5 = (f32[2,3,3,1,18,130]{5,3,4,2,1,0:T(1,128)S(1)}, f32[2,3,3,1,18,130]{5,3,4,2,1,0:T(1,128)S(1)}, u32[]{:S(2)}, u32[]{:S(2)}) collective-permute-start(f32[2,3,3,1,18,130]{5,3,4,2,1,0:T(1,128)S(1)} %get-tuple-element.13), channel_id=1, source_target_pairs={{1,0},{3,2},{5,4},{7,6},{9,8},{11,10},{13,12},{15,14},{17,16},{19,... | collective-permute-start | bytes 505448 | tf_op jit(solution)/shard_map/ppermute | solution.py:25
  355.4 23.1 %collective-permute-start.8 = (f32[32,18,1]{2,0,1:T(8,128)S(1)}, f32[32,18,1]{2,0,1:T(8,128)S(1)}, u32[]{:S(2)}, u32[]{:S(2)}) collective-permute-start(f32[32,18,1]{2,0,1:T(8,128)S(1)} %get-tuple-element.43), channel_id=1, source_target_pairs={{2,0},{4,2},{6,4},{8,6},{10,8},{12,10},{14,12},{3,1},{5,3},{7,5},{... | collective-permute-start | bytes 6920 | tf_op jit(solution)/shard_map/ppermute | solution.py:25
  356.7 21.8 %collective-permute-start.9 = (f32[32,18,1]{2,0,1:T(8,128)S(1)}, f32[32,18,1]{2,0,1:T(8,128)S(1)}, u32[]{:S(2)}, u32[]{:S(2)}) collective-permute-start(f32[32,18,1]{2,0,1:T(8,128)S(1)} %get-tuple-element.42), channel_id=1, source_target_pairs={{0,2},{2,4},{4,6},{6,8},{8,10},{10,12},{12,14},{1,3},{3,5},{5,7},{... | collective-permute-start | bytes 6920 | tf_op jit(solution)/shard_map/ppermute | solution.py:22
  378.5 2.0 copy-start.4
  378.5 2.0 copy-start.5
  378.7 12.4 %collective-permute-start.10 = (f32[1,18,130]{2,0,1:T(1,128)S(1)}, f32[1,18,130]{2,0,1:T(1,128)S(1)}, u32[]{:S(2)}, u32[]{:S(2)}) collective-permute-start(f32[1,18,130]{2,0,1:T(1,128)S(1)} %get-tuple-element.30), channel_id=1, source_target_pairs={{1,0},{3,2},{5,4},{7,6},{9,8},{11,10},{13,12},{15,14},{17,16},{19,... | collective-permute-start | bytes 28088 | tf_op jit(solution)/shard_map/ppermute | solution.py:25
  380.6 10.5 %collective-permute-start.11 = (f32[1,18,130]{2,0,1:T(1,128)S(1)}, f32[1,18,130]{2,0,1:T(1,128)S(1)}, u32[]{:S(2)}, u32[]{:S(2)}) collective-permute-start(f32[1,18,130]{2,0,1:T(1,128)S(1)} %get-tuple-element.31), channel_id=1, source_target_pairs={{0,1},{2,3},{4,5},{6,7},{8,9},{10,11},{12,13},{14,15},{16,17},{18,... | collective-permute-start | bytes 28088 | tf_op jit(solution)/shard_map/ppermute | solution.py:22
  394.2 5.4 %collective-permute-start.12 = (f32[32,1,128]{2,0,1:T(8,128)S(1)}, f32[32,1,128]{2,0,1:T(8,128)S(1)}, u32[]{:S(2)}, u32[]{:S(2)}) collective-permute-start(f32[32,1,128]{2,0,1:T(8,128)S(1)} %get-tuple-element.47), channel_id=1, source_target_pairs={{16,0},{32,16},{48,32},{64,48},{80,64},{96,80},{112,96},{128,112},... | collective-permute-start | bytes 49160 | tf_op jit(solution)/shard_map/ppermute | solution.py:25
  395.5 49.0 %copy-start.7 = (f32[3,32,16,128]{3,2,1,0:T(8,128)S(1)}, f32[3,32,16,128]{3,2,1,0:T(8,128)}, u32[]{:S(2)}) copy-start(f32[3,32,16,128]{3,2,1,0:T(8,128)} %param.11) | copy-start | bytes 2359300
  395.5 5.0 collective-permute-start.13
  400.7 8.2 %collective-permute-start.14 = (f32[32,18,1]{2,0,1:T(8,128)S(1)}, f32[32,18,1]{2,0,1:T(8,128)S(1)}, u32[]{:S(2)}, u32[]{:S(2)}) collective-permute-start(f32[32,18,1]{2,0,1:T(8,128)S(1)} %get-tuple-element.41), channel_id=1, source_target_pairs={{2,0},{4,2},{6,4},{8,6},{10,8},{12,10},{14,12},{3,1},{5,3},{7,5},{... | collective-permute-start | bytes 6920 | tf_op jit(solution)/shard_map/ppermute | solution.py:25
  402.0 7.6 %collective-permute-start.15 = (f32[32,18,1]{2,0,1:T(8,128)S(1)}, f32[32,18,1]{2,0,1:T(8,128)S(1)}, u32[]{:S(2)}, u32[]{:S(2)}) collective-permute-start(f32[32,18,1]{2,0,1:T(8,128)S(1)} %get-tuple-element.40), channel_id=1, source_target_pairs={{0,2},{2,4},{4,6},{6,8},{8,10},{10,12},{12,14},{1,3},{3,5},{5,7},{... | collective-permute-start | bytes 6920 | tf_op jit(solution)/shard_map/ppermute | solution.py:22
  409.8 6.8 %collective-permute-start.16 = (f32[1,18,130]{2,0,1:T(1,128)S(1)}, f32[1,18,130]{2,0,1:T(1,128)S(1)}, u32[]{:S(2)}, u32[]{:S(2)}) collective-permute-start(f32[1,18,130]{2,0,1:T(1,128)S(1)} %get-tuple-element.28), channel_id=1, source_target_pairs={{1,0},{3,2},{5,4},{7,6},{9,8},{11,10},{13,12},{15,14},{17,16},{19,... | collective-permute-start | bytes 28088 | tf_op jit(solution)/shard_map/ppermute | solution.py:25
  415.3 3.1 collective-permute-start.17
  421.1 5.7 %collective-permute-start.18 = (f32[32,1,128]{2,0,1:T(8,128)S(1)}, f32[32,1,128]{2,0,1:T(8,128)S(1)}, u32[]{:S(2)}, u32[]{:S(2)}) collective-permute-start(f32[32,1,128]{2,0,1:T(8,128)S(1)} %get-tuple-element.45), channel_id=1, source_target_pairs={{16,0},{32,16},{48,32},{64,48},{80,64},{96,80},{112,96},{128,112},... | collective-permute-start | bytes 49160 | tf_op jit(solution)/shard_map/ppermute | solution.py:25
  422.4 5.2 collective-permute-start.19
  427.8 10.5 %collective-permute-start.20 = (f32[32,18,1]{2,0,1:T(8,128)S(1)}, f32[32,18,1]{2,0,1:T(8,128)S(1)}, u32[]{:S(2)}, u32[]{:S(2)}) collective-permute-start(f32[32,18,1]{2,0,1:T(8,128)S(1)} %get-tuple-element.39), channel_id=1, source_target_pairs={{2,0},{4,2},{6,4},{8,6},{10,8},{12,10},{14,12},{3,1},{5,3},{7,5},{... | collective-permute-start | bytes 6920 | tf_op jit(solution)/shard_map/ppermute | solution.py:25
  429.1 10.1 %collective-permute-start.21 = (f32[32,18,1]{2,0,1:T(8,128)S(1)}, f32[32,18,1]{2,0,1:T(8,128)S(1)}, u32[]{:S(2)}, u32[]{:S(2)}) collective-permute-start(f32[32,18,1]{2,0,1:T(8,128)S(1)} %get-tuple-element.38), channel_id=1, source_target_pairs={{0,2},{2,4},{4,6},{6,8},{8,10},{10,12},{12,14},{1,3},{3,5},{5,7},{... | collective-permute-start | bytes 6920 | tf_op jit(solution)/shard_map/ppermute | solution.py:22
  439.4 5.2 collective-permute-start.22
  443.2 3.1 collective-permute-start.23
  449.1 21.5 %all-to-all-start.1 = ((f32[32,16,128]{2,0,1:T(8,128)}), f32[32,16,128]{2,0,1:T(8,128)S(1)}, u32[]{:S(2)}, u32[]{:S(2)}) async-start(f32[32,16,128]{2,0,1:T(8,128)} %get-tuple-element.8), calls=%async_computation.1 | async-start | bytes 524288 | tf_op jit(solution)/shard_map/all_to_all | solution.py:86
  477.1 29.2 %all-to-all-start.2 = ((f32[128,1,512]{2,1,0:T(1,128)}), f32[128,1,512]{2,1,0:T(1,128)S(1)}, u32[]{:S(2)}, u32[]{:S(2)}) async-start(f32[128,1,512]{2,1,0:T(1,128)} %reshape.202), calls=%async_computation.2 | async-start | bytes 524288 | tf_op jit(solution)/shard_map/all_to_all | solution.py:98
Sparse Core Ops, SparseCore 0:
  37.5 213.6 all-reduce.4
